TPU v7x, 32 devices: a whole 2x2x4 slice. The times are simulated.
32 devices in a mesh: grp: 2 (over x), ctr: 16 (over z, y, core).
Axes of the slice: x: 2, y: 2, z: 4, core: 2. Of those that a mesh axis runs over, the one named last changes fastest.
Arguments:
- centres: bfloat16 [6144, 768], P(('grp', 'ctr')), parts along dimension 0
- sample_idx: int32 [1024], P(('grp', 'ctr')), parts along dimension 0, may hold values from 0 to 3071, as said below
- coef: float32 [6144], P(('grp', 'ctr')), parts along dimension 0
- metric_factor: bfloat16 [768, 768], replicated, may hold values from -0.21875 to 0.21875
Outputs:
- metric_new: float32 [1536, 768], P(('grp', 'ctr')), parts along dimension 0
- transformed: float32 [1024, 768], P(('grp', 'ctr')), parts along dimension 0
There are 2 independent parts, one for each index of `grp`. A program takes and returns all parts, laid end to end along the dimension named above; an argument that names none is the same for every part. Nothing has to cross between parts.
Inputs may be any that keep to these rules, and one draw needn't show every extreme that they name: The 32 samples of the k-th aligned block of sample_idx are distinct centres of the k-th block of 192 centres.
All inputs are finite; a program needn't handle non-finite values.
Results may differ from a plain program's by a relative error of at most 0.0031.
Values may be sent and summed in bfloat16 or wider, within the bound.
A program may use at most 128 MiB of HBM per device.

v0:
```python
import jax
import jax.numpy as jnp
from jax import lax
from jax.sharding import PartitionSpec as P


def block_grad(rows_u, v_own, sv_own, coef):
    width = rows_u.shape[1]
    su = jnp.sum(rows_u.astype(jnp.float32) ** 2, axis=1)
    cross = jnp.dot(rows_u, v_own.T, preferred_element_type=jnp.float32)
    dist_sq = jnp.maximum(su[:, None] + sv_own[None, :] - 2.0 * cross, 0.0)
    radius = jnp.sqrt(dist_sq / width + 1.0)
    weight = coef[None, :] * jnp.exp(-radius / 4.0) / (4.0 * width * radius)
    wround = weight.astype(jnp.bfloat16)
    return jnp.dot(wround, v_own, preferred_element_type=jnp.float32) - jnp.sum(weight, axis=1)[
        :, None
    ] * rows_u.astype(jnp.float32)


def local(centres, sample_idx, coef, metric_factor):
    width = centres.shape[1]
    own_count = sample_idx.shape[0]
    devices = lax.axis_size("ctr")
    offset = lax.axis_index("ctr") * centres.shape[0]
    own_rows = jnp.take(centres, sample_idx - offset, axis=0)
    u_own = jnp.dot(own_rows, metric_factor, preferred_element_type=jnp.float32).astype(
        jnp.bfloat16
    )
    v_own = jnp.dot(centres, metric_factor, preferred_element_type=jnp.float32).astype(jnp.bfloat16)
    factor = metric_factor.astype(jnp.float32)
    coef_full = lax.all_gather(coef, "ctr", axis=0, tiled=True)
    piece = lax.all_gather(v_own, "ctr", axis=0, tiled=True)
    sv_piece = jnp.sum(piece.astype(jnp.float32) ** 2, axis=1)
    summed = block_grad(u_own, piece, sv_piece, coef_full)
    grads = jnp.dot(summed, factor.T, precision=lax.Precision.HIGHEST)
    local_outer = jnp.dot(grads.T, grads, precision=lax.Precision.HIGHEST) / (own_count * devices)
    agop = lax.psum(local_outer, "ctr")
    metric_full = agop * width / jnp.trace(agop)
    row_count = width // devices
    metric_rows = lax.dynamic_slice_in_dim(
        metric_full, lax.axis_index("ctr") * row_count, row_count, 0
    )
    transformed = jnp.dot(grads, metric_full, precision=lax.Precision.HIGHEST)
    return (metric_rows, transformed)


def solution(mesh):
    placed = (P(("grp", "ctr"), None), P(("grp", "ctr")), P(("grp", "ctr")), P())
    return jax.shard_map(
        local,
        mesh=mesh,
        in_specs=placed,
        out_specs=(P(("grp", "ctr"), None), P(("grp", "ctr"), None)),
        check_vma=False,
    )
```

profile of v0, /device:TPU:0, one launch (start us, length us, event | category | flops | bytes accessed | tf_op | source)
XLA Modules:
  0.0 199.3 jit_solution(7842170020570275571)
XLA Ops:
  7.2 0.0 all-gather.2.cloned.1.call-start
  7.2 1.2 copy-done
  8.4 2.1 %convolution_convert_fusion = bf16[192,768]{1,0:T(8,128)(2,1)} fusion(bf16[192,768]{1,0:T(8,128)(2,1)} %param.4, bf16[768,768]{1,0:T(8,128)(2,1)S(1)} %copy-done), kind=kOutput, calls=%fused_computation.12 | convolution fusion | flops 226639872 | bytes 1769472 | tf_op jit(solution)/shard_map/dot_general | solution.py:29
  10.5 0.0 all-gather.2.cloned.1.call-update
  10.5 0.0 all-reduce.3.cloned.1.call-start
  10.6 0.7 compare_and_fusion
  11.3 1.7 gather_fusion
  12.9 0.6 dynamic-slice
  14.2 0.3 dynamic-update-slice
  14.5 64.2 %all-reduce = f32[3072]{0:T(1024)S(1)} all-reduce(f32[3072]{0:T(1024)S(1)} %dynamic-update-slice), channel_id=1, replica_groups=mesh['grp'=2,'ctr'=16] {'ctr'}, use_global_device_ids=true, to_apply=%add | all-reduce | flops 3072 | bytes 24576
  78.7 0.5 fusion.6
  79.1 0.0 all-gather.2.cloned.1.call-done
  79.2 3.5 %multiply_reduce_fusion = f32[3072]{0:T(1024)S(1)} fusion(bf16[3072,768]{1,0:T(8,128)(2,1)} %all-gather.2.cloned.1.call-done), kind=kLoop, calls=%fused_computation.1 | loop fusion | flops 7074816 | bytes 4730880 | tf_op jit(solution)/shard_map/reduce_sum | solution.py:33
  82.7 0.3 copy-done.1
  82.9 1.7 fusion.11
  84.6 0.9 convolution_subtract_fusion
  85.4 1.1 fusion.12
  86.6 3.5 %convolution_multiply_fusion.1 = f32[768,768]{1,0:T(8,128)} fusion(f32[32,768]{1,0:T(8,128)S(1)} %fusion.12), kind=kOutput, calls=%fused_computation.11 | convolution fusion | flops 227082240 | bytes 2457600 | tf_op jit(solution)/shard_map/dot_general | solution.py:36
  90.1 0.0 all-reduce.3.cloned.1.call-update
  90.1 96.2 %all-reduce.3.cloned.1.call-done = f32[768,768]{1,0:T(8,128)} async-done(((f32[768,768]{1,0:T(8,128)}), f32[768,768]{1,0:T(8,128)}) %all-reduce.3.cloned.1.call-update) | async-done | bytes 2359312 | tf_op jit(solution)/shard_map/psum | solution.py:37
  186.3 2.5 %select_reduce_fusion = f32[]{:T(128)} fusion(f32[768,768]{1,0:T(8,128)} %all-reduce.3.cloned.1.call-done), kind=kLoop, calls=%fused_computation.8 | loop fusion | flops 1769471 | bytes 2359300 | tf_op jit(solution)/shard_map/jit(trace)/reduce_sum | solution.py:38
  188.8 0.8 multiply_divide_fusion
  189.7 2.1 %fusion.13 = f32[32,768]{1,0:T(8,128)} fusion(f32[32,768]{1,0:T(8,128)S(1)} %fusion.12, f32[768,768]{1,0:T(8,128)S(1)} %multiply_divide_fusion), kind=kOutput, calls=%fused_computation.30 | convolution fusion | flops 226492416 | bytes 2555904 | tf_op jit(solution)/shard_map/dot_general | solution.py:43
  191.7 0.7 constant_dynamic-slice_fusion
  (10 shorter events, 0.0 us)
Async XLA Ops:
  7.2 1.3 copy-start
  7.2 5.8 %copy-start.4 = (u32[32]{0:T(128)S(1)}, u32[32]{0:T(128)}, u32[]{:S(2)}) copy-start(u32[32]{0:T(128)} %constant.52) | copy-start | bytes 388
  7.2 7.0 %copy-start.3 = (f32[192]{0:T(256)S(1)}, f32[192]{0:T(256)}, u32[]{:S(2)}) copy-start(f32[192]{0:T(256)} %param.6) | copy-start | bytes 2308
  7.2 72.0 %all-gather.2.cloned.1.call-start = ((), (), s32[]{:S(2)}) async-start(), calls=%async_computation | async-start | bytes 5013504 | tf_op jit(solution)/shard_map/all_gather | solution.py:32
  10.5 175.8 %all-reduce.3.cloned.1.call-start = ((), (), s32[]{:S(2)}) async-start(), calls=%async_computation.1 | async-start | bytes 4718592 | tf_op jit(solution)/shard_map/psum | solution.py:37
  79.2 3.8 %copy-start.1 = (bf16[3072,768]{1,0:T(8,128)(2,1)S(1)}, bf16[3072,768]{1,0:T(8,128)(2,1)}, u32[]{:S(2)}) copy-start(bf16[3072,768]{1,0:T(8,128)(2,1)} %all-gather.2.cloned.1.call-done) | copy-start | bytes 14155780
  186.3 2.5 %copy-start.2 = (f32[768,768]{1,0:T(8,128)S(1)}, f32[768,768]{1,0:T(8,128)}, u32[]{:S(2)}) copy-start(f32[768,768]{1,0:T(8,128)} %all-reduce.3.cloned.1.call-done) | copy-start | bytes 7077892
Sparse Core Ops, SparseCore 0:
  10.7 56.3 all-gather.1
  90.2 96.0 all-reduce.2
where the time goes:
time: 200 us; the launch traced here: 199 us
  waiting for transfers between devices  96.3 us (48%)
  blocking collectives  64.2 us (32%)
  between operations  14.8 us (7%)
  matrix products  11.8 us (6%)
  other arithmetic  7.48 us (4%)
  local copies, waits for them, and re-layouts  4.68 us (2%)
    psum x1, waiting for transfers between devices, local(): agop = lax.psum(local_outer, 'ctr')  96.2 us
    unnamed x1, blocking collectives  64.2 us
  transfers between devices with their start and end apart: 2, of which 1 were waited for; matrix products, arithmetic and copies ran while one was open for 2% of the time, Pallas kernels for 0%

commit v1 on v0

--- a/solution.py
+++ b/solution.py
@@ -34,7 +34,7 @@
     summed = block_grad(u_own, piece, sv_piece, coef_full)
     grads = jnp.dot(summed, factor.T, precision=lax.Precision.HIGHEST)
     local_outer = jnp.dot(grads.T, grads, precision=lax.Precision.HIGHEST) / (own_count * devices)
-    agop = lax.psum(local_outer, "ctr")
+    agop = jnp.sum(lax.all_gather(local_outer, "ctr"), axis=0)
     metric_full = agop * width / jnp.trace(agop)
     row_count = width // devices
     metric_rows = lax.dynamic_slice_in_dim(

time: 200 us -> 300 us (1.50)
  waiting for transfers between devices: 96.3 us -> 185 us
  other arithmetic: 7.48 us -> 19.4 us
    all_gather x0 -> x1, waiting for transfers between devices: none -> 185 us  [local(): agop = jnp.sum(lax.all_gather(local_outer, 'ctr'), axis=0)]
    psum x1 -> x0, waiting for transfers between devices: 96.2 us -> none  [local(): agop = lax.psum(local_outer, 'ctr')]
    reduce_sum x0 -> x1, other arithmetic: none -> 13.7 us  [local(): agop = jnp.sum(lax.all_gather(local_outer, 'ctr'), axis=0)]
  transfers between devices with their start and end apart: 2 -> 2, of which waited for: 1 -> 1; matrix products, arithmetic and copies ran while one was open for 2% -> 1% of each run, Pallas kernels for 0% -> 0%
where the time goes in v1:
time: 300 us
  waiting for transfers between devices  185 us (62%)
  blocking collectives  64.6 us (22%)
  other arithmetic  19.4 us (6%)
  between operations  14.8 us (5%)
  matrix products  11.8 us (4%)
  local copies, waits for them, and re-layouts  4.45 us (1%)
    all_gather x1, waiting for transfers between devices, local(): agop = jnp.sum(lax.all_gather(local_outer, 'ctr'), axis=0)  185 us
    unnamed x1, blocking collectives  64.6 us
    reduce_sum x1, other arithmetic, local(): agop = jnp.sum(lax.all_gather(local_outer, 'ctr'), axis=0)  13.7 us
  transfers between devices with their start and end apart: 2, of which 1 were waited for; matrix products, arithmetic and copies ran while one was open for 1% of the time, Pallas kernels for 0%

profile of v1, /device:TPU:0, one launch (start us, length us, event | category | flops | bytes accessed | tf_op | source)
XLA Modules:
  0.0 300.0 jit_solution(10525340048923902765)
XLA Ops:
  7.2 0.0 all-gather.4.cloned.1.call-start
  7.3 1.3 copy-done
  8.5 2.1 convolution_convert_fusion
  10.6 0.0 all-gather.6.cloned.1.call-start
  10.7 0.7 compare_and_fusion
  11.4 0.6 gather_fusion
  12.0 0.6 dynamic-slice
  13.3 0.3 dynamic-update-slice
  13.6 64.6 %all-reduce = f32[3072]{0:T(1024)S(1)} all-reduce(f32[3072]{0:T(1024)S(1)} %dynamic-update-slice), channel_id=1, replica_groups=mesh['grp'=2,'ctr'=16] {'ctr'}, use_global_device_ids=true, to_apply=%add | all-reduce | flops 3072 | bytes 24576
  78.1 0.5 fusion.6
  78.6 3.5 %multiply_reduce_fusion = f32[3072]{0:T(1024)S(1)} fusion(bf16[3072,768]{1,0:T(8,128)(2,1)} %all-gather.4.cloned.1.call-done), kind=kLoop, calls=%fused_computation.1 | loop fusion | flops 7074816 | bytes 4730880 | tf_op jit(solution)/shard_map/reduce_sum | solution.py:33
  82.1 0.3 copy-done.1
  82.4 1.6 fusion.11
  84.0 0.9 convolution_subtract_fusion
  84.9 1.1 fusion.12
  86.0 0.7 copy-done.3
  86.7 3.5 %convolution_multiply_fusion.1 = f32[768,768]{1,0:T(8,128)} fusion(f32[32,768]{1,0:T(8,128)S(1)} %fusion.12), kind=kOutput, calls=%fused_computation.11 | convolution fusion | flops 227082240 | bytes 2457600 | tf_op jit(solution)/shard_map/dot_general | solution.py:36
  90.2 184.9 %all-gather.6.cloned.1.call-done = f32[12288,768]{1,0:T(8,128)} async-done(((f32[768,768]{1,0:T(8,128)}), f32[12288,768]{1,0:T(8,128)}) %all-gather.6.cloned.1.call-update) | async-done | bytes 37748752 | tf_op jit(solution)/shard_map/all_gather | solution.py:37
  275.1 13.7 %reduce_sum.49 = f32[768,768]{1,0:T(8,128)S(1)} reduce(f32[16,768,768]{2,1,0:T(8,128)} %bitcast.15, f32[]{:T(128)} %constant.20.clone.1), dimensions={0}, to_apply=%region_3.4 | reduce | flops 8847360 | bytes 40108036 | tf_op jit(solution)/shard_map/reduce_sum | solution.py:37
  288.8 0.7 select_reduce_fusion
  289.5 0.8 multiply_divide_fusion
  290.3 0.1 copy-done.4
  290.4 2.1 fusion.13
  292.5 0.7 constant_dynamic-slice_fusion
  (15 shorter events, 0.1 us)
Async XLA Ops:
  7.2 1.4 copy-start
  7.2 4.8 %copy-start.6 = (u32[32]{0:T(128)S(1)}, u32[32]{0:T(128)}, u32[]{:S(2)}) copy-start(u32[32]{0:T(128)} %constant.52) | copy-start | bytes 388
  7.2 4.2 %copy-start.2 = (bf16[192,768]{1,0:T(8,128)(2,1)S(1)}, bf16[192,768]{1,0:T(8,128)(2,1)}, u32[]{:S(2)}) copy-start(bf16[192,768]{1,0:T(8,128)(2,1)} %param.4) | copy-start | bytes 884740
  7.2 6.1 %copy-start.5 = (f32[192]{0:T(256)S(1)}, f32[192]{0:T(256)}, u32[]{:S(2)}) copy-start(f32[192]{0:T(256)} %param.6) | copy-start | bytes 2308
  7.2 71.4 %all-gather.4.cloned.1.call-start = ((), (), s32[]{:S(2)}) async-start(), calls=%async_computation | async-start | bytes 5013504 | tf_op jit(solution)/shard_map/all_gather | solution.py:32
  10.6 264.4 %all-gather.6.cloned.1.call-start = ((), (), s32[]{:S(2)}) async-start(), calls=%async_computation.1 | async-start | bytes 40108032 | tf_op jit(solution)/shard_map/all_gather | solution.py:37
  78.6 3.8 %copy-start.1 = (bf16[3072,768]{1,0:T(8,128)(2,1)S(1)}, bf16[3072,768]{1,0:T(8,128)(2,1)}, u32[]{:S(2)}) copy-start(bf16[3072,768]{1,0:T(8,128)(2,1)} %all-gather.4.cloned.1.call-done) | copy-start | bytes 14155780
  86.0 0.7 copy-start.3
  289.5 0.9 copy-start.4
Sparse Core Ops, SparseCore 0:
  10.7 56.1 all-gather.3
  90.3 184.7 all-gather.5
